TPU v7x, 512 devices: a whole 4x8x8 slice. The times are simulated.
512 devices in a mesh: ctx: 64 (over z_hi, y, core), tp: 8 (over x, z_lo).
Axes of the slice: x: 4, y: 8, z: 8 (z_hi: 4, z_lo: 2; z = z_hi * 2 + z_lo), core: 2. Of those that a mesh axis runs over, the one named last changes fastest.
Arguments:
- query_in: bfloat16 [1024, 16384], P('tp', 'ctx'), may hold values from -6 to 6
- key_in: bfloat16 [1024, 16384], P('tp', 'ctx'), may hold values from -6 to 6
- value_in: bfloat16 [1024, 16384], P('tp', 'ctx'), may hold values from -6 to 6
- short_kernel: float32 [3, 1024, 7], P(None, 'tp'), may hold values from -2 to 2
- basis_weight: float32 [64, 33], replicated, may hold values from -96 to 96
- basis_bias: float32 [64], replicated, may hold values from -3.140625 to 3.140625
- filter_proj: float32 [1024, 64], P('tp'), may hold values from -0.75 to 0.75
- decay_rate: float32 [1024], P('tp'), as said below
- skip_gain: float32 [1024], P('tp'), may hold values from -3 to 3
- grad_out: bfloat16 [1024, 16384], P('tp', 'ctx'), may hold values from -6 to 6
Outputs:
- mixed: bfloat16 [1024, 16384], P('tp', 'ctx')
- grad_query: bfloat16 [1024, 16384], P('tp', 'ctx')
- grad_key: bfloat16 [1024, 16384], P('tp', 'ctx')
- grad_value: bfloat16 [1024, 16384], P('tp', 'ctx')
- grad_proj: float32 [1024, 64], P('tp')
- grad_basis: float32 [64, 33], replicated
Inputs may be any that keep to these rules, and one draw needn't show every extreme that they name: decay_rate is positive in every channel.
All inputs are finite; a program needn't handle non-finite values.
Results may differ from a plain program's by a relative error of at most 0.0066.
Values may be sent and summed in bfloat16 or wider, within the bound.
No kernel may reach another device: no remote copies, remote signals or barrier semaphores. Data moves between devices by JAX's collectives and lax.ppermute only.
A program may use at most 64 MiB of HBM per device.

v0:
```python
import math
import jax
import jax.numpy as jnp
from jax import lax
from jax.sharding import PartitionSpec as P

PRECISE = lax.Precision.HIGHEST


def passed_along(value, axis, steps):
    count = lax.axis_size(axis)
    leading, last = (max(0, -steps), min(count, count - steps))
    return lax.ppermute(value, axis, [(source, source + steps) for source in range(leading, last)])


def features(offset_pos, num_pos, seq_total, num_freq):
    positions = offset_pos + jnp.arange(num_pos, dtype=jnp.int32)
    pieces = [positions.astype(jnp.float32) / seq_total]
    for harmonic in range(1, num_freq + 1):
        angles = (harmonic * positions % seq_total).astype(jnp.float32) * (
            2.0 * math.pi / seq_total
        )
        pieces.append(jnp.cos(angles))
        pieces.append(jnp.sin(angles))
    return jnp.stack(pieces)


def window(decay_rate, offset_pos, num_pos, seq_total):
    positions = (offset_pos + jnp.arange(num_pos, dtype=jnp.int32)).astype(jnp.float32)
    energy = jnp.expm1(-2.0 * decay_rate) / jnp.expm1(-2.0 * decay_rate / seq_total)
    return (
        jnp.exp(-(decay_rate[:, None] * positions[None, :]) / seq_total) / jnp.sqrt(energy)[:, None]
    )


def featurize_rim(signal, before, kernel):
    extended = jnp.concatenate([before, signal], axis=1).astype(jnp.float32)
    num_taps = kernel.shape[1]
    rim_len = num_taps - 1
    num_tok = signal.shape[1]
    result = kernel[:, 0:1] * extended[:, rim_len:]
    for offset in range(1, num_taps):
        result = (
            result
            + kernel[:, offset : offset + 1]
            * extended[:, rim_len - offset : rim_len - offset + num_tok]
        )
    return result


def featurize_back(signal, following, kernel):
    extended = jnp.concatenate([signal, following], axis=1).astype(jnp.float32)
    num_taps = kernel.shape[1]
    num_tok = signal.shape[1]
    result = kernel[:, 0:1] * extended[:, :num_tok]
    for offset in range(1, num_taps):
        result = result + kernel[:, offset : offset + 1] * extended[:, offset : offset + num_tok]
    return result


def tables(num_rows, num_cols, modulus):
    row_ids = jnp.arange(num_rows, dtype=jnp.int32)[:, None]
    col_ids = jnp.arange(num_cols, dtype=jnp.int32)[None, :]
    angles = (row_ids * col_ids % modulus).astype(jnp.float32) * (-2.0 * math.pi / modulus)
    return (jnp.cos(angles), jnp.sin(angles))


def spectrum(signal, outer, twiddle, inner):
    num_chan = signal.shape[0]
    folded = signal.reshape(num_chan, outer[0].shape[1], inner[0].shape[0])
    section_re = jnp.einsum("kt,nts->nks", outer[0], folded, precision=PRECISE)
    section_im = jnp.einsum("kt,nts->nks", outer[1], folded, precision=PRECISE)
    turned_re = section_re * twiddle[0] - section_im * twiddle[1]
    turned_im = section_re * twiddle[1] + section_im * twiddle[0]
    spec_re = jnp.einsum("nks,sj->nkj", turned_re, inner[0], precision=PRECISE) - jnp.einsum(
        "nks,sj->nkj", turned_im, inner[1], precision=PRECISE
    )
    spec_im = jnp.einsum("nks,sj->nkj", turned_re, inner[1], precision=PRECISE) + jnp.einsum(
        "nks,sj->nkj", turned_im, inner[0], precision=PRECISE
    )
    return (spec_re, spec_im)


def restore(spec_re, spec_im, outer, twiddle, inner):
    num_chan = spec_re.shape[0]
    padded_len = outer[0].shape[0] * inner[0].shape[0]
    back_re = jnp.einsum("nkj,sj->nks", spec_re, inner[0], precision=PRECISE) + jnp.einsum(
        "nkj,sj->nks", spec_im, inner[1], precision=PRECISE
    )
    back_im = jnp.einsum("nkj,sj->nks", spec_im, inner[0], precision=PRECISE) - jnp.einsum(
        "nkj,sj->nks", spec_re, inner[1], precision=PRECISE
    )
    turned_re = back_re * twiddle[0] + back_im * twiddle[1]
    turned_im = back_im * twiddle[0] - back_re * twiddle[1]
    result = jnp.einsum("kt,nks->nts", outer[0], turned_re, precision=PRECISE) + jnp.einsum(
        "kt,nks->nts", outer[1], turned_im, precision=PRECISE
    )
    return result.reshape(num_chan, -1) * (1.0 / padded_len)


def convolve_forward(carried_chan, filter_chan, own_skip, transform_tables):
    outer, twiddle, inner = transform_tables
    carried_wide = carried_chan.astype(jnp.float32)
    carried_re, carried_im = spectrum(carried_wide, outer, twiddle, inner)
    filter_re, filter_im = spectrum(filter_chan.astype(jnp.float32), outer, twiddle, inner)
    conv_chan = restore(
        filter_re * carried_re - filter_im * carried_im,
        filter_re * carried_im + filter_im * carried_re,
        outer,
        twiddle,
        inner,
    )
    long_chan = (conv_chan + own_skip[:, None] * carried_wide).astype(jnp.bfloat16)
    return (long_chan, (carried_re, carried_im, filter_re, filter_im))


def convolve_backward(grad_chan, spectra, own_skip, transform_tables):
    outer, twiddle, inner = transform_tables
    carried_re, carried_im, filter_re, filter_im = spectra
    grad_chan_wide = grad_chan.astype(jnp.float32)
    grad_re, grad_im = spectrum(grad_chan_wide, outer, twiddle, inner)
    carried_grad_chan = (
        restore(
            filter_re * grad_re + filter_im * grad_im,
            filter_re * grad_im - filter_im * grad_re,
            outer,
            twiddle,
            inner,
        )
        + own_skip[:, None] * grad_chan_wide
    ).astype(jnp.bfloat16)
    filter_grad_chan = restore(
        carried_re * grad_re + carried_im * grad_im,
        carried_re * grad_im - carried_im * grad_re,
        outer,
        twiddle,
        inner,
    ).astype(jnp.bfloat16)
    return (carried_grad_chan, filter_grad_chan)


def on_device(
    query_in,
    key_in,
    value_in,
    short_kernel,
    basis_weight,
    basis_bias,
    filter_proj,
    decay_rate,
    skip_gain,
    grad_out,
):
    ctx_size = lax.axis_size("ctx")
    ctx_rank = lax.axis_index("ctx")
    tp_size = lax.axis_size("tp")
    num_tok = query_in.shape[1]
    chan_local = query_in.shape[0]
    seq_total = num_tok * ctx_size
    all_channels = chan_local * tp_size
    num_freq = (basis_weight.shape[1] - 1) // 2
    feat_width = basis_weight.shape[0]
    rim_len = short_kernel.shape[2] - 1
    tok_start = ctx_rank * num_tok
    rim_edge = num_tok - rim_len
    per_dev = chan_local // ctx_size
    chan_start = ctx_rank * per_dev
    own_skip = lax.dynamic_slice_in_dim(skip_gain, chan_start, per_dev)
    proj_scale = 1.0 / math.sqrt(seq_total)
    basis_scale = math.sqrt(feat_width / (seq_total * all_channels))
    before = passed_along(
        (query_in[:, rim_edge:], key_in[:, rim_edge:], value_in[:, rim_edge:]), "ctx", 1
    )
    query_feat = featurize_rim(query_in, before[0], short_kernel[0])
    key_feat = featurize_rim(key_in, before[1], short_kernel[1])
    value_feat = featurize_rim(value_in, before[2], short_kernel[2])
    carried = (key_feat * value_feat).astype(jnp.bfloat16)
    grad_wide = grad_out.astype(jnp.float32)
    grad_long = (grad_wide * query_feat).astype(jnp.bfloat16)
    basis_rows = features(tok_start, num_tok, seq_total, num_freq)
    hidden_in = (
        jnp.dot(basis_weight, basis_rows, precision=PRECISE, preferred_element_type=jnp.float32)
        + basis_bias[:, None]
    )
    activation = jnp.sin(hidden_in)
    envelope = window(decay_rate, tok_start, num_tok, seq_total)
    filter_tok = (
        jnp.dot(filter_proj, activation, precision=PRECISE, preferred_element_type=jnp.float32)
        * envelope
    ).astype(jnp.bfloat16)
    inner_len = 2 * ctx_size
    transform_tables = (
        tables(num_tok, num_tok // 2, num_tok),
        tables(num_tok, inner_len, 2 * seq_total),
        tables(inner_len, inner_len, inner_len),
    )
    spread = (
        lax.all_to_all(carried, "ctx", split_axis=0, concat_axis=1, tiled=True),
        lax.all_to_all(filter_tok, "ctx", split_axis=0, concat_axis=1, tiled=True),
    )
    carried_chan = spread[0]
    filter_chan = spread[1]
    long_chan, spectra = convolve_forward(carried_chan, filter_chan, own_skip, transform_tables)
    long_tok = lax.all_to_all(long_chan, "ctx", split_axis=1, concat_axis=0, tiled=True)
    grad_chan = lax.all_to_all(grad_long, "ctx", split_axis=0, concat_axis=1, tiled=True)
    carried_grad_chan, filter_grad_chan = convolve_backward(
        grad_chan, spectra, own_skip, transform_tables
    )
    returned = (
        lax.all_to_all(carried_grad_chan, "ctx", split_axis=1, concat_axis=0, tiled=True),
        lax.all_to_all(filter_grad_chan, "ctx", split_axis=1, concat_axis=0, tiled=True),
    )
    carried_grad = returned[0]
    filter_grad_tok = returned[1]
    long_wide = long_tok.astype(jnp.float32)
    mixed = (query_feat * long_wide).astype(jnp.bfloat16)
    grad_query_feat = (grad_wide * long_wide).astype(jnp.bfloat16)
    grad_raw = filter_grad_tok.astype(jnp.float32) * envelope
    part_proj = jnp.dot(
        grad_raw, activation.T, precision=PRECISE, preferred_element_type=jnp.float32
    )
    grad_hidden = jnp.dot(
        filter_proj.T, grad_raw, precision=PRECISE, preferred_element_type=jnp.float32
    ) * jnp.cos(hidden_in)
    part_basis = jnp.dot(
        grad_hidden, basis_rows.T, precision=PRECISE, preferred_element_type=jnp.float32
    )
    grad_proj = lax.psum(part_proj, "ctx") * proj_scale
    grad_basis = lax.psum(part_basis, ("ctx", "tp")) * basis_scale
    carried_grad_wide = carried_grad.astype(jnp.float32)
    grad_key_feat = (carried_grad_wide * value_feat).astype(jnp.bfloat16)
    grad_value_feat = (carried_grad_wide * key_feat).astype(jnp.bfloat16)
    following = passed_along(
        (grad_query_feat[:, :rim_len], grad_key_feat[:, :rim_len], grad_value_feat[:, :rim_len]),
        "ctx",
        -1,
    )
    grad_query = featurize_back(grad_query_feat, following[0], short_kernel[0]).astype(jnp.bfloat16)
    grad_key = featurize_back(grad_key_feat, following[1], short_kernel[1]).astype(jnp.bfloat16)
    grad_value = featurize_back(grad_value_feat, following[2], short_kernel[2]).astype(jnp.bfloat16)
    return (mixed, grad_query, grad_key, grad_value, grad_proj, grad_basis)


def solution(mesh):
    return jax.shard_map(
        on_device,
        mesh=mesh,
        in_specs=(
            P("tp", "ctx"),
            P("tp", "ctx"),
            P("tp", "ctx"),
            P(None, "tp", None),
            P(),
            P(),
            P("tp", None),
            P("tp"),
            P("tp"),
            P("tp", "ctx"),
        ),
        out_specs=(
            P("tp", "ctx"),
            P("tp", "ctx"),
            P("tp", "ctx"),
            P("tp", "ctx"),
            P("tp", None),
            P(),
        ),
        check_vma=False,
    )
```

profile of v0, /device:TPU:1, one launch (start us, length us, event | category | flops | bytes accessed | tf_op | source)
XLA Modules:
  0.0 538.5 jit_solution(8369667688324918726)
XLA Ops:
  0.6 0.8 slice.242
  1.5 4.6 collective-permute-start
  10.4 15.5 %all-to-all-start = ((bf16[64,2,256]{2,1,0:T(2,128)(2,1)}), bf16[64,2,256]{2,1,0:T(2,128)(2,1)S(1)}, u32[]{:S(2)}, u32[]{:S(2)}) async-start(bf16[64,2,256]{2,1,0:T(2,128)(2,1)} %all_to_all.60), calls=%async_computation | async-start | bytes 131072 | tf_op jit(solution)/shard_map/all_to_all | solution.py:199
  26.0 3.5 collective-permute-start.2
  29.6 2.2 collective-permute-start.1
  35.7 2.4 all-to-all-done
  38.1 9.7 %all-to-all-start.3 = ((bf16[64,2,256]{2,1,0:T(2,128)(2,1)}), bf16[64,2,256]{2,1,0:T(2,128)(2,1)S(1)}, u32[]{:S(2)}, u32[]{:S(2)}) async-start(bf16[64,2,256]{2,1,0:T(2,128)(2,1)} %all_to_all.67), calls=%async_computation.3 | async-start | bytes 131072 | tf_op jit(solution)/shard_map/all_to_all | solution.py:205
  51.7 7.9 %all-to-all-done.3 = bf16[64,2,256]{2,1,0:T(2,128)(2,1)S(1)} async-done(((bf16[64,2,256]{2,1,0:T(2,128)(2,1)}), bf16[64,2,256]{2,1,0:T(2,128)(2,1)S(1)}, u32[]{:S(2)}, u32[]{:S(2)}) %all-to-all-start.3) | async-done | bytes 65568 | tf_op jit(solution)/shard_map/all_to_all | solution.py:205
  60.4 0.8 convolution_bitcast_fusion.1
  67.6 11.5 %fusion.19 = f32[2,128,128]{2,1,0:T(8,128)S(1)} fusion(f32[2,256,128]{1,2,0:T(8,128)S(1)} %convolution_subtract_fusion.1, f32[2,256,128]{1,2,0:T(8,128)S(1)} %convolution_add_fusion.1, f32[256,128]{0,1:T(8,128)S(1)} %copy.206, f32[256,128]{0,1:T(8,128)S(1)} %copy.204), kind=kOutput, calls=%fused_computation.45 | convolution fusion | flops 101318656 | bytes 917504 | tf_op jit(solution)/shard_map/kt,nks->nts/dot_general | solution.py:95
  79.1 0.9 fusion.2
  80.9 4.8 all-to-all-start.4
  86.0 12.0 %all-to-all-done.4 = bf16[2,64,256]{2,0,1:T(2,128)(2,1)S(1)} async-done(((bf16[2,64,256]{2,0,1:T(2,128)(2,1)}), bf16[2,64,256]{2,0,1:T(2,128)(2,1)S(1)}, u32[]{:S(2)}, u32[]{:S(2)}) %all-to-all-start.4) | async-done | bytes 65568 | tf_op jit(solution)/shard_map/all_to_all | solution.py:210
  98.5 2.3 collective-permute-start.5
  101.9 6.0 %all-to-all-start.1 = ((bf16[64,2,256]{2,1,0:T(2,128)(2,1)}), bf16[64,2,256]{2,1,0:T(2,128)(2,1)S(1)}, u32[]{:S(2)}, u32[]{:S(2)}) async-start(bf16[64,2,256]{2,1,0:T(2,128)(2,1)} %all_to_all.63), calls=%async_computation.1 | async-start | bytes 131072 | tf_op jit(solution)/shard_map/all_to_all | solution.py:198
  108.0 2.4 collective-permute-start.4
  110.4 1.0 fusion.37
  111.4 2.1 collective-permute-done.4
  113.5 1.0 fusion.44
  114.5 5.6 %all-to-all-done.1 = bf16[64,2,256]{2,1,0:T(2,128)(2,1)S(1)} async-done(((bf16[64,2,256]{2,1,0:T(2,128)(2,1)}), bf16[64,2,256]{2,1,0:T(2,128)(2,1)S(1)}, u32[]{:S(2)}, u32[]{:S(2)}) %all-to-all-start.1) | async-done | bytes 65568 | tf_op jit(solution)/shard_map/all_to_all | solution.py:198
  124.0 0.8 multiply_add_fusion
  127.4 0.9 fusion.12
  128.3 0.9 fusion.8
  130.0 7.0 %all-to-all-start.5 = ((bf16[2,64,256]{2,0,1:T(2,128)(2,1)}), bf16[2,64,256]{2,0,1:T(2,128)(2,1)S(1)}, u32[]{:S(2)}, u32[]{:S(2)}) async-start(bf16[2,64,256]{2,0,1:T(2,128)(2,1)} %copy.242), calls=%async_computation.5 | async-start | bytes 131072 | tf_op jit(solution)/shard_map/all_to_all | solution.py:211
  139.6 0.9 fusion.26
  140.5 0.9 fusion.4
  142.3 6.9 %all-to-all-done.5 = bf16[2,64,256]{2,0,1:T(2,128)(2,1)S(1)} async-done(((bf16[2,64,256]{2,0,1:T(2,128)(2,1)}), bf16[2,64,256]{2,0,1:T(2,128)(2,1)S(1)}, u32[]{:S(2)}, u32[]{:S(2)}) %all-to-all-start.5) | async-done | bytes 65568 | tf_op jit(solution)/shard_map/all_to_all | solution.py:211
  149.2 5.8 %all-to-all-start.2 = ((bf16[2,64,256]{2,0,1:T(2,128)(2,1)}), bf16[2,64,256]{2,0,1:T(2,128)(2,1)S(1)}, u32[]{:S(2)}, u32[]{:S(2)}) async-start(bf16[2,64,256]{2,0,1:T(2,128)(2,1)} %copy.223), calls=%async_computation.2 | async-start | bytes 131072 | tf_op jit(solution)/shard_map/all_to_all | solution.py:204
  156.2 99.6 %psum.15 = f32[64,33]{0,1:T(8,128)S(1)} all-reduce(f32[64,33]{0,1:T(8,128)S(1)} %fusion.423), channel_id=1, replica_groups=mesh['ctx'=64,'tp'=8] {'ctx','tp'}, use_global_device_ids=true, to_apply=%region_1.2 | all-reduce | flops 2112 | bytes 16896 | tf_op jit(solution)/shard_map/psum | solution.py:229
  255.8 270.7 %psum.14 = f32[128,64]{0,1:T(8,128)S(1)} all-reduce(f32[128,64]{0,1:T(8,128)S(1)} %fusion.417), channel_id=1, replica_groups=mesh['ctx'=64,'tp'=8] {'ctx'}, use_global_device_ids=true, to_apply=%region_0.1 | all-reduce | flops 8192 | bytes 65536 | tf_op jit(solution)/shard_map/psum | solution.py:228
  528.0 8.4 %collective-permute-start.3 = (bf16[128,6]{1,0:T(8,128)(2,1)S(1)}, bf16[128,6]{1,0:T(8,128)(2,1)S(1)}, u32[]{:S(2)}, u32[]{:S(2)}) collective-permute-start(bf16[128,6]{1,0:T(8,128)(2,1)S(1)} %slice.333), channel_id=1, source_target_pairs={{8,0},{16,8},{24,16},{32,24},{40,32},{48,40},{56,48},{64,56},{72,6... | collective-permute-start | bytes 4616 | tf_op jit(solution)/shard_map/ppermute | solution.py:13
  537.3 1.0 fusion.51
  (132 shorter events, 36.1 us)
Async XLA Ops:
  0.6 8.8 %copy-start = (f32[128,64]{0,1:T(8,128)S(1)}, f32[128,64]{0,1:T(8,128)}, u32[]{:S(2)}) copy-start(f32[128,64]{0,1:T(8,128)} %param.16) | copy-start | bytes 98308
  1.5 32.3 %collective-permute-start = (bf16[128,6]{1,0:T(8,128)(2,1)S(1)}, bf16[128,6]{1,0:T(8,128)(2,1)S(1)}, u32[]{:S(2)}, u32[]{:S(2)}) collective-permute-start(bf16[128,6]{1,0:T(8,128)(2,1)S(1)} %slice.242), channel_id=1, source_target_pairs={{0,8},{8,16},{16,24},{24,32},{32,40},{40,48},{48,56},{56,64},{64,7... | collective-permute-start | bytes 4616 | tf_op jit(solution)/shard_map/ppermute | solution.py:13
  7.5 0.7 copy-start.9
  8.2 0.7 copy-start.5
  8.2 0.7 copy-start.7
  10.4 15.5 %copy-start.3 = (bf16[128,256]{1,0:T(8,128)(2,1)S(1)}, bf16[128,256]{1,0:T(8,128)(2,1)}, u32[]{:S(2)}) copy-start(bf16[128,256]{1,0:T(8,128)(2,1)} %param.12) | copy-start | bytes 196612
  10.4 27.7 %all-to-all-start = ((bf16[64,2,256]{2,1,0:T(2,128)(2,1)}), bf16[64,2,256]{2,1,0:T(2,128)(2,1)S(1)}, u32[]{:S(2)}, u32[]{:S(2)}) async-start(bf16[64,2,256]{2,1,0:T(2,128)(2,1)} %all_to_all.60), calls=%async_computation | async-start | bytes 131072 | tf_op jit(solution)/shard_map/all_to_all | solution.py:199
  25.9 3.6 copy-start.4
  26.0 59.8 %collective-permute-start.2 = (bf16[128,6]{1,0:T(8,128)(2,1)S(1)}, bf16[128,6]{1,0:T(8,128)(2,1)S(1)}, u32[]{:S(2)}, u32[]{:S(2)}) collective-permute-start(bf16[128,6]{1,0:T(8,128)(2,1)S(1)} %slice.274), channel_id=1, source_target_pairs={{0,8},{8,16},{16,24},{24,32},{32,40},{40,48},{48,56},{56,64},{64,7... | collective-permute-start | bytes 4616 | tf_op jit(solution)/shard_map/ppermute | solution.py:13
  29.6 2.7 copy-start.6
  29.6 56.3 %collective-permute-start.1 = (bf16[128,6]{1,0:T(8,128)(2,1)S(1)}, bf16[128,6]{1,0:T(8,128)(2,1)S(1)}, u32[]{:S(2)}, u32[]{:S(2)}) collective-permute-start(bf16[128,6]{1,0:T(8,128)(2,1)S(1)} %slice.258), channel_id=1, source_target_pairs={{0,8},{8,16},{16,24},{24,32},{32,40},{40,48},{48,56},{56,64},{64,7... | collective-permute-start | bytes 4616 | tf_op jit(solution)/shard_map/ppermute | solution.py:13
  33.0 0.9 copy-start.2
  33.1 0.7 copy-start.8
  33.8 0.8 copy-start.1
  38.1 21.5 %all-to-all-start.3 = ((bf16[64,2,256]{2,1,0:T(2,128)(2,1)}), bf16[64,2,256]{2,1,0:T(2,128)(2,1)S(1)}, u32[]{:S(2)}, u32[]{:S(2)}) async-start(bf16[64,2,256]{2,1,0:T(2,128)(2,1)} %all_to_all.67), calls=%async_computation.3 | async-start | bytes 131072 | tf_op jit(solution)/shard_map/all_to_all | solution.py:205
  80.9 17.0 %all-to-all-start.4 = ((bf16[2,64,256]{2,0,1:T(2,128)(2,1)}), bf16[2,64,256]{2,0,1:T(2,128)(2,1)S(1)}, u32[]{:S(2)}, u32[]{:S(2)}) async-start(bf16[2,64,256]{2,0,1:T(2,128)(2,1)} %copy.236), calls=%async_computation.4 | async-start | bytes 131072 | tf_op jit(solution)/shard_map/all_to_all | solution.py:210
  98.5 11.8 %collective-permute-start.5 = (bf16[128,6]{1,0:T(8,128)(2,1)S(1)}, bf16[128,6]{1,0:T(8,128)(2,1)S(1)}, u32[]{:S(2)}, u32[]{:S(2)}) collective-permute-start(bf16[128,6]{1,0:T(8,128)(2,1)S(1)} %slice.349), channel_id=1, source_target_pairs={{8,0},{16,8},{24,16},{32,24},{40,32},{48,40},{56,48},{64,56},{72,6... | collective-permute-start | bytes 4616 | tf_op jit(solution)/shard_map/ppermute | solution.py:13
  101.9 18.2 %all-to-all-start.1 = ((bf16[64,2,256]{2,1,0:T(2,128)(2,1)}), bf16[64,2,256]{2,1,0:T(2,128)(2,1)S(1)}, u32[]{:S(2)}, u32[]{:S(2)}) async-start(bf16[64,2,256]{2,1,0:T(2,128)(2,1)} %all_to_all.63), calls=%async_computation.1 | async-start | bytes 131072 | tf_op jit(solution)/shard_map/all_to_all | solution.py:198
  108.0 5.5 %collective-permute-start.4 = (bf16[128,6]{1,0:T(8,128)(2,1)S(1)}, bf16[128,6]{1,0:T(8,128)(2,1)S(1)}, u32[]{:S(2)}, u32[]{:S(2)}) collective-permute-start(bf16[128,6]{1,0:T(8,128)(2,1)S(1)} %slice.341), channel_id=1, source_target_pairs={{8,0},{16,8},{24,16},{32,24},{40,32},{48,40},{56,48},{64,56},{72,6... | collective-permute-start | bytes 4616 | tf_op jit(solution)/shard_map/ppermute | solution.py:13
  130.0 19.1 %all-to-all-start.5 = ((bf16[2,64,256]{2,0,1:T(2,128)(2,1)}), bf16[2,64,256]{2,0,1:T(2,128)(2,1)S(1)}, u32[]{:S(2)}, u32[]{:S(2)}) async-start(bf16[2,64,256]{2,0,1:T(2,128)(2,1)} %copy.242), calls=%async_computation.5 | async-start | bytes 131072 | tf_op jit(solution)/shard_map/all_to_all | solution.py:211
  149.2 378.0 %all-to-all-start.2 = ((bf16[2,64,256]{2,0,1:T(2,128)(2,1)}), bf16[2,64,256]{2,0,1:T(2,128)(2,1)S(1)}, u32[]{:S(2)}, u32[]{:S(2)}) async-start(bf16[2,64,256]{2,0,1:T(2,128)(2,1)} %copy.223), calls=%async_computation.2 | async-start | bytes 131072 | tf_op jit(solution)/shard_map/all_to_all | solution.py:204
  528.0 9.3 %collective-permute-start.3 = (bf16[128,6]{1,0:T(8,128)(2,1)S(1)}, bf16[128,6]{1,0:T(8,128)(2,1)S(1)}, u32[]{:S(2)}, u32[]{:S(2)}) collective-permute-start(bf16[128,6]{1,0:T(8,128)(2,1)S(1)} %slice.333), channel_id=1, source_target_pairs={{8,0},{16,8},{24,16},{32,24},{40,32},{48,40},{56,48},{64,56},{72,6... | collective-permute-start | bytes 4616 | tf_op jit(solution)/shard_map/ppermute | solution.py:13
where the time goes:
time: 544 us; the launch traced here: 539 us
  blocking collectives  370 us (68%)
  starting transfers between devices  72.2 us (13%)
  matrix products  39.1 us (7%)
  waiting for transfers between devices  37.1 us (7%)
  other arithmetic  9.16 us (2%)
  local copies, waits for them, and re-layouts  8.96 us (2%)
    psum x1, blocking collectives, on_device(): grad_proj = lax.psum(part_proj, 'ctx') * proj_scale  271 us
    psum x1, blocking collectives, on_device(): grad_basis = lax.psum(part_basis, ('ctx', 'tp')) * basis_scale  99.6 us
    ppermute x6, starting transfers between devices, passed_along(): lax.ppermute(value, axis, [(source, source + steps) for source in range(l...  23.4 us
    all_to_all x1, starting transfers between devices, on_device(): lax.all_to_all(filter_tok, 'ctx', split_axis=0, concat_axis=1, tiled=True)  15.5 us
    dot_general x3, matrix products, restore(): jnp.einsum('kt,nks->nts', outer[0], turned_re, precision=PRECISE)  13.3 us
    all_to_all x1, waiting for transfers between devices, on_device(): lax.all_to_all(carried_grad_chan, 'ctx', split_axis=1, concat_axis=0, til...  12 us
  transfers between devices with their start and end apart: 12, of which 7 were waited for; matrix products, arithmetic and copies ran while one was open for 7% of the time, Pallas kernels for 0%

commit v1 on v0

--- a/solution.py
+++ b/solution.py
@@ -226,7 +226,7 @@
         grad_hidden, basis_rows.T, precision=PRECISE, preferred_element_type=jnp.float32
     )
     grad_proj = lax.psum(part_proj, "ctx") * proj_scale
-    grad_basis = lax.psum(part_basis, ("ctx", "tp")) * basis_scale
+    grad_basis = lax.psum(lax.psum(part_basis, "ctx"), "tp") * basis_scale
     carried_grad_wide = carried_grad.astype(jnp.float32)
     grad_key_feat = (carried_grad_wide * value_feat).astype(jnp.bfloat16)
     grad_value_feat = (carried_grad_wide * key_feat).astype(jnp.bfloat16)

time: 544 us -> 484 us (0.89)
  blocking collectives: 370 us -> 303 us
  starting transfers between devices: 72.2 us -> 79.2 us
    psum x1, blocking collectives: 99.6 us -> 27.4 us  [on_device(): grad_basis = lax.psum(lax.psum(part_basis, 'ctx'), 'tp') * basis_scale]
    ppermute x6, starting transfers between devices: 23.4 us -> 30.4 us  [passed_along(): lax.ppermute(value, axis, [(source, source + steps) for source in range(l...]
  transfers between devices with their start and end apart: 12 -> 12, of which waited for: 7 -> 7; matrix products, arithmetic and copies ran while one was open for 7% -> 8% of each run, Pallas kernels for 0% -> 0%
where the time goes in v1:
time: 484 us; the launch traced here: 478 us
  blocking collectives  303 us (63%)
  starting transfers between devices  79.2 us (16%)
  matrix products  39.1 us (8%)
  waiting for transfers between devices  37.1 us (8%)
  other arithmetic  9.16 us (2%)
  local copies, waits for them, and re-layouts  8.96 us (2%)
    psum x1, blocking collectives, on_device(): grad_proj = lax.psum(part_proj, 'ctx') * proj_scale  276 us
    ppermute x6, starting transfers between devices, passed_along(): lax.ppermute(value, axis, [(source, source + steps) for source in range(l...  30.4 us
    psum x1, blocking collectives, on_device(): grad_basis = lax.psum(lax.psum(part_basis, 'ctx'), 'tp') * basis_scale  27.4 us
    all_to_all x1, starting transfers between devices, on_device(): lax.all_to_all(filter_tok, 'ctx', split_axis=0, concat_axis=1, tiled=True)  15.5 us
    dot_general x3, matrix products, restore(): jnp.einsum('kt,nks->nts', outer[0], turned_re, precision=PRECISE)  13.3 us
    all_to_all x1, waiting for transfers between devices, on_device(): lax.all_to_all(carried_grad_chan, 'ctx', split_axis=1, concat_axis=0, til...  12 us
  transfers between devices with their start and end apart: 12, of which 7 were waited for; matrix products, arithmetic and copies ran while one was open for 8% of the time, Pallas kernels for 0%

profile of v1, /device:TPU:1, one launch (start us, length us, event | category | flops | bytes accessed | tf_op | source)
XLA Modules:
  0.0 478.1 jit_solution(12756111540021453274)
XLA Ops:
  0.6 0.8 slice.242
  1.5 4.6 collective-permute-start
  10.4 15.5 %all-to-all-start = ((bf16[64,2,256]{2,1,0:T(2,128)(2,1)}), bf16[64,2,256]{2,1,0:T(2,128)(2,1)S(1)}, u32[]{:S(2)}, u32[]{:S(2)}) async-start(bf16[64,2,256]{2,1,0:T(2,128)(2,1)} %all_to_all.60), calls=%async_computation | async-start | bytes 131072 | tf_op jit(solution)/shard_map/all_to_all | solution.py:199
  26.0 3.5 collective-permute-start.2
  29.6 2.2 collective-permute-start.1
  35.7 2.4 all-to-all-done
  38.1 9.7 %all-to-all-start.3 = ((bf16[64,2,256]{2,1,0:T(2,128)(2,1)}), bf16[64,2,256]{2,1,0:T(2,128)(2,1)S(1)}, u32[]{:S(2)}, u32[]{:S(2)}) async-start(bf16[64,2,256]{2,1,0:T(2,128)(2,1)} %all_to_all.67), calls=%async_computation.3 | async-start | bytes 131072 | tf_op jit(solution)/shard_map/all_to_all | solution.py:205
  51.7 7.9 %all-to-all-done.3 = bf16[64,2,256]{2,1,0:T(2,128)(2,1)S(1)} async-done(((bf16[64,2,256]{2,1,0:T(2,128)(2,1)}), bf16[64,2,256]{2,1,0:T(2,128)(2,1)S(1)}, u32[]{:S(2)}, u32[]{:S(2)}) %all-to-all-start.3) | async-done | bytes 65568 | tf_op jit(solution)/shard_map/all_to_all | solution.py:205
  60.4 0.8 convolution_bitcast_fusion.1
  67.6 11.5 %fusion.19 = f32[2,128,128]{2,1,0:T(8,128)S(1)} fusion(f32[2,256,128]{1,2,0:T(8,128)S(1)} %convolution_subtract_fusion.1, f32[2,256,128]{1,2,0:T(8,128)S(1)} %convolution_add_fusion.1, f32[256,128]{0,1:T(8,128)S(1)} %copy.206, f32[256,128]{0,1:T(8,128)S(1)} %copy.204), kind=kOutput, calls=%fused_computation.45 | convolution fusion | flops 101318656 | bytes 917504 | tf_op jit(solution)/shard_map/kt,nks->nts/dot_general | solution.py:95
  79.1 0.9 fusion.2
  80.9 4.8 %all-to-all-start.4 = ((bf16[2,64,256]{2,0,1:T(2,128)(2,1)}), bf16[2,64,256]{2,0,1:T(2,128)(2,1)S(1)}, u32[]{:S(2)}, u32[]{:S(2)}) async-start(bf16[2,64,256]{2,0,1:T(2,128)(2,1)} %copy.236), calls=%async_computation.4 | async-start | bytes 131072 | tf_op jit(solution)/shard_map/all_to_all | solution.py:210
  86.0 12.0 %all-to-all-done.4 = bf16[2,64,256]{2,0,1:T(2,128)(2,1)S(1)} async-done(((bf16[2,64,256]{2,0,1:T(2,128)(2,1)}), bf16[2,64,256]{2,0,1:T(2,128)(2,1)S(1)}, u32[]{:S(2)}, u32[]{:S(2)}) %all-to-all-start.4) | async-done | bytes 65568 | tf_op jit(solution)/shard_map/all_to_all | solution.py:210
  98.5 2.3 collective-permute-start.5
  101.9 6.0 %all-to-all-start.1 = ((bf16[64,2,256]{2,1,0:T(2,128)(2,1)}), bf16[64,2,256]{2,1,0:T(2,128)(2,1)S(1)}, u32[]{:S(2)}, u32[]{:S(2)}) async-start(bf16[64,2,256]{2,1,0:T(2,128)(2,1)} %all_to_all.63), calls=%async_computation.1 | async-start | bytes 131072 | tf_op jit(solution)/shard_map/all_to_all | solution.py:198
  108.0 2.4 collective-permute-start.4
  110.4 1.0 fusion.37
  111.4 2.1 collective-permute-done.4
  113.5 1.0 fusion.44
  114.5 5.6 %all-to-all-done.1 = bf16[64,2,256]{2,1,0:T(2,128)(2,1)S(1)} async-done(((bf16[64,2,256]{2,1,0:T(2,128)(2,1)}), bf16[64,2,256]{2,1,0:T(2,128)(2,1)S(1)}, u32[]{:S(2)}, u32[]{:S(2)}) %all-to-all-start.1) | async-done | bytes 65568 | tf_op jit(solution)/shard_map/all_to_all | solution.py:198
  124.0 0.8 multiply_add_fusion
  127.4 0.9 fusion.12
  128.3 0.9 fusion.8
  130.0 7.0 %all-to-all-start.5 = ((bf16[2,64,256]{2,0,1:T(2,128)(2,1)}), bf16[2,64,256]{2,0,1:T(2,128)(2,1)S(1)}, u32[]{:S(2)}, u32[]{:S(2)}) async-start(bf16[2,64,256]{2,0,1:T(2,128)(2,1)} %copy.242), calls=%async_computation.5 | async-start | bytes 131072 | tf_op jit(solution)/shard_map/all_to_all | solution.py:211
  139.6 0.9 fusion.26
  140.5 0.9 fusion.4
  142.3 6.9 %all-to-all-done.5 = bf16[2,64,256]{2,0,1:T(2,128)(2,1)S(1)} async-done(((bf16[2,64,256]{2,0,1:T(2,128)(2,1)}), bf16[2,64,256]{2,0,1:T(2,128)(2,1)S(1)}, u32[]{:S(2)}, u32[]{:S(2)}) %all-to-all-start.5) | async-done | bytes 65568 | tf_op jit(solution)/shard_map/all_to_all | solution.py:211
  149.2 5.8 %all-to-all-start.2 = ((bf16[2,64,256]{2,0,1:T(2,128)(2,1)}), bf16[2,64,256]{2,0,1:T(2,128)(2,1)S(1)}, u32[]{:S(2)}, u32[]{:S(2)}) async-start(bf16[2,64,256]{2,0,1:T(2,128)(2,1)} %copy.223), calls=%async_computation.2 | async-start | bytes 131072 | tf_op jit(solution)/shard_map/all_to_all | solution.py:204
  156.2 275.6 %all-reduce = (f32[128,64]{0,1:T(8,128)S(1)}, f32[64,33]{0,1:T(8,128)S(1)}) all-reduce(f32[128,64]{0,1:T(8,128)S(1)} %fusion.417, f32[64,33]{0,1:T(8,128)S(1)} %fusion.423), channel_id=1, replica_groups=mesh['ctx'=64,'tp'=8] {'ctx'}, use_global_device_ids=true, to_apply=%region_0.1 | all-reduce | flops 10304 | bytes 82432 | tf_op jit(solution)/shard_map/psum | solution.py:228
  431.8 27.4 %psum.23 = f32[64,33]{0,1:T(8,128)S(1)} all-reduce(f32[64,33]{0,1:T(8,128)S(1)} %get-tuple-element.7), channel_id=1, replica_groups=mesh['ctx'=64,'tp'=8] {'tp'}, use_global_device_ids=true, to_apply=%region_2.3 | all-reduce | flops 2112 | bytes 16896 | tf_op jit(solution)/shard_map/psum | solution.py:229
  460.6 15.5 %collective-permute-start.3 = (bf16[128,6]{1,0:T(8,128)(2,1)S(1)}, bf16[128,6]{1,0:T(8,128)(2,1)S(1)}, u32[]{:S(2)}, u32[]{:S(2)}) collective-permute-start(bf16[128,6]{1,0:T(8,128)(2,1)S(1)} %slice.333), channel_id=1, source_target_pairs={{8,0},{16,8},{24,16},{32,24},{40,32},{48,40},{56,48},{64,56},{72,6... | collective-permute-start | bytes 4616 | tf_op jit(solution)/shard_map/ppermute | solution.py:13
  476.9 1.0 fusion.51
  (132 shorter events, 36.1 us)
Async XLA Ops:
  0.6 8.8 %copy-start = (f32[128,64]{0,1:T(8,128)S(1)}, f32[128,64]{0,1:T(8,128)}, u32[]{:S(2)}) copy-start(f32[128,64]{0,1:T(8,128)} %param.16) | copy-start | bytes 98308
  1.5 32.3 %collective-permute-start = (bf16[128,6]{1,0:T(8,128)(2,1)S(1)}, bf16[128,6]{1,0:T(8,128)(2,1)S(1)}, u32[]{:S(2)}, u32[]{:S(2)}) collective-permute-start(bf16[128,6]{1,0:T(8,128)(2,1)S(1)} %slice.242), channel_id=1, source_target_pairs={{0,8},{8,16},{16,24},{24,32},{32,40},{40,48},{48,56},{56,64},{64,7... | collective-permute-start | bytes 4616 | tf_op jit(solution)/shard_map/ppermute | solution.py:13
  7.5 0.7 copy-start.9
  8.2 0.7 copy-start.5
  8.2 0.7 copy-start.7
  10.4 15.5 %copy-start.3 = (bf16[128,256]{1,0:T(8,128)(2,1)S(1)}, bf16[128,256]{1,0:T(8,128)(2,1)}, u32[]{:S(2)}) copy-start(bf16[128,256]{1,0:T(8,128)(2,1)} %param.12) | copy-start | bytes 196612
  10.4 27.7 %all-to-all-start = ((bf16[64,2,256]{2,1,0:T(2,128)(2,1)}), bf16[64,2,256]{2,1,0:T(2,128)(2,1)S(1)}, u32[]{:S(2)}, u32[]{:S(2)}) async-start(bf16[64,2,256]{2,1,0:T(2,128)(2,1)} %all_to_all.60), calls=%async_computation | async-start | bytes 131072 | tf_op jit(solution)/shard_map/all_to_all | solution.py:199
  25.9 3.6 copy-start.4
  26.0 59.8 %collective-permute-start.2 = (bf16[128,6]{1,0:T(8,128)(2,1)S(1)}, bf16[128,6]{1,0:T(8,128)(2,1)S(1)}, u32[]{:S(2)}, u32[]{:S(2)}) collective-permute-start(bf16[128,6]{1,0:T(8,128)(2,1)S(1)} %slice.274), channel_id=1, source_target_pairs={{0,8},{8,16},{16,24},{24,32},{32,40},{40,48},{48,56},{56,64},{64,7... | collective-permute-start | bytes 4616 | tf_op jit(solution)/shard_map/ppermute | solution.py:13
  29.6 2.7 copy-start.6
  29.6 56.3 %collective-permute-start.1 = (bf16[128,6]{1,0:T(8,128)(2,1)S(1)}, bf16[128,6]{1,0:T(8,128)(2,1)S(1)}, u32[]{:S(2)}, u32[]{:S(2)}) collective-permute-start(bf16[128,6]{1,0:T(8,128)(2,1)S(1)} %slice.258), channel_id=1, source_target_pairs={{0,8},{8,16},{16,24},{24,32},{32,40},{40,48},{48,56},{56,64},{64,7... | collective-permute-start | bytes 4616 | tf_op jit(solution)/shard_map/ppermute | solution.py:13
  33.0 0.9 copy-start.2
  33.1 0.7 copy-start.8
  33.8 0.8 copy-start.1
  38.1 21.5 %all-to-all-start.3 = ((bf16[64,2,256]{2,1,0:T(2,128)(2,1)}), bf16[64,2,256]{2,1,0:T(2,128)(2,1)S(1)}, u32[]{:S(2)}, u32[]{:S(2)}) async-start(bf16[64,2,256]{2,1,0:T(2,128)(2,1)} %all_to_all.67), calls=%async_computation.3 | async-start | bytes 131072 | tf_op jit(solution)/shard_map/all_to_all | solution.py:205
  80.9 17.0 %all-to-all-start.4 = ((bf16[2,64,256]{2,0,1:T(2,128)(2,1)}), bf16[2,64,256]{2,0,1:T(2,128)(2,1)S(1)}, u32[]{:S(2)}, u32[]{:S(2)}) async-start(bf16[2,64,256]{2,0,1:T(2,128)(2,1)} %copy.236), calls=%async_computation.4 | async-start | bytes 131072 | tf_op jit(solution)/shard_map/all_to_all | solution.py:210
  98.5 11.8 %collective-permute-start.5 = (bf16[128,6]{1,0:T(8,128)(2,1)S(1)}, bf16[128,6]{1,0:T(8,128)(2,1)S(1)}, u32[]{:S(2)}, u32[]{:S(2)}) collective-permute-start(bf16[128,6]{1,0:T(8,128)(2,1)S(1)} %slice.349), channel_id=1, source_target_pairs={{8,0},{16,8},{24,16},{32,24},{40,32},{48,40},{56,48},{64,56},{72,6... | collective-permute-start | bytes 4616 | tf_op jit(solution)/shard_map/ppermute | solution.py:13
  101.9 18.2 %all-to-all-start.1 = ((bf16[64,2,256]{2,1,0:T(2,128)(2,1)}), bf16[64,2,256]{2,1,0:T(2,128)(2,1)S(1)}, u32[]{:S(2)}, u32[]{:S(2)}) async-start(bf16[64,2,256]{2,1,0:T(2,128)(2,1)} %all_to_all.63), calls=%async_computation.1 | async-start | bytes 131072 | tf_op jit(solution)/shard_map/all_to_all | solution.py:198
  108.0 5.5 %collective-permute-start.4 = (bf16[128,6]{1,0:T(8,128)(2,1)S(1)}, bf16[128,6]{1,0:T(8,128)(2,1)S(1)}, u32[]{:S(2)}, u32[]{:S(2)}) collective-permute-start(bf16[128,6]{1,0:T(8,128)(2,1)S(1)} %slice.341), channel_id=1, source_target_pairs={{8,0},{16,8},{24,16},{32,24},{40,32},{48,40},{56,48},{64,56},{72,6... | collective-permute-start | bytes 4616 | tf_op jit(solution)/shard_map/ppermute | solution.py:13
  130.0 19.1 %all-to-all-start.5 = ((bf16[2,64,256]{2,0,1:T(2,128)(2,1)}), bf16[2,64,256]{2,0,1:T(2,128)(2,1)S(1)}, u32[]{:S(2)}, u32[]{:S(2)}) async-start(bf16[2,64,256]{2,0,1:T(2,128)(2,1)} %copy.242), calls=%async_computation.5 | async-start | bytes 131072 | tf_op jit(solution)/shard_map/all_to_all | solution.py:211
  149.2 310.6 %all-to-all-start.2 = ((bf16[2,64,256]{2,0,1:T(2,128)(2,1)}), bf16[2,64,256]{2,0,1:T(2,128)(2,1)S(1)}, u32[]{:S(2)}, u32[]{:S(2)}) async-start(bf16[2,64,256]{2,0,1:T(2,128)(2,1)} %copy.223), calls=%async_computation.2 | async-start | bytes 131072 | tf_op jit(solution)/shard_map/all_to_all | solution.py:204
  460.6 16.3 %collective-permute-start.3 = (bf16[128,6]{1,0:T(8,128)(2,1)S(1)}, bf16[128,6]{1,0:T(8,128)(2,1)S(1)}, u32[]{:S(2)}, u32[]{:S(2)}) collective-permute-start(bf16[128,6]{1,0:T(8,128)(2,1)S(1)} %slice.333), channel_id=1, source_target_pairs={{8,0},{16,8},{24,16},{32,24},{40,32},{48,40},{56,48},{64,56},{72,6... | collective-permute-start | bytes 4616 | tf_op jit(solution)/shard_map/ppermute | solution.py:13
